TPU v7x, 32 devices: a whole 2x2x4 slice. The times are simulated.
32 devices in a mesh: elem: 16 (over z, x, core), band: 2 (over y).
Axes of the slice: x: 2, y: 2, z: 4, core: 2. Of those that a mesh axis runs over, the one named last changes fastest.
Arguments:
- basis: bfloat16 [256, 32, 16, 160], P('band', 'elem'), may hold values from -8 to 8
- hamiltonian: bfloat16 [32, 16, 7, 160, 160], P('elem'), may hold values from -0.09375 to 0.09375
- neighbours: int32 [32, 16, 6], P('elem'), may hold values from 0 to 511, as said below
Outputs:
- filtered: bfloat16 [256, 32, 16, 160], P('band', 'elem')
- intersection: float32 [256, 256], P('elem', 'band')
- projected: float32 [256, 256], P('elem', 'band')
Inputs may be any that keep to these rules, and one draw needn't show every extreme that they name: neighbours[z, s, d] = z2 * 16 + s2 names the element (z2, s2) that shares face d with element (z, s) on a periodic grid of 4 x 4 x 32 cells, whose cells are stored within each layer in an order of the draw; faces 0 to 3 lie in the same layer z, face 4 in layer z - 1 and face 5 in layer z + 1, both modulo 32.
All inputs are finite; a program needn't handle non-finite values.
Results may differ from a plain program's by a relative error of at most 0.0075.
Values may be sent and summed in bfloat16 or wider, within the bound.
A program may use at most 64 MiB of HBM per device.

v0:
```python
import functools

import jax
import jax.numpy as jnp
from jax import lax
from jax.experimental import pallas as pl
from jax.experimental.pallas import tpu as pltpu
from jax.sharding import PartitionSpec as P

DEGREE = 4
FAR = 2
LATE = 2
MESH = pl.DeviceIdType.MESH
F32 = jnp.float32
BF16 = jnp.bfloat16


def dot(a, b):
    return jnp.dot(a, b, preferred_element_type=F32)


def kernel(
    geom,
    nbr,
    y0,
    ham_hbm,
    f_out,
    s_out,
    p_out,
    ham,
    buf_a,
    buf_b,
    near0,
    near1,
    far0,
    far1,
    acc,
    ft,
    it,
    others,
    parts,
    got1,
    mid,
    got2,
    ham_sem,
    out_sem,
    near_send,
    near_recv,
    far_send,
    far_recv,
    fsend,
    frecv,
    r1send,
    r1recv,
    r2send,
    r2recv,
):
    n, nband, cells, n1, n2, rows, factor = geom
    total = 2 * cells
    funcs, bands = y0.shape[1], y0.shape[2]
    me = lax.axis_index("elem")
    bme = lax.axis_index("band")
    right, left = lax.rem(me + 1, n), lax.rem(me + n - 1, n)
    group, member = me // n1, me % n1

    hcopies = []
    hparts = ham_sem.shape[0]
    for c in range(hparts):
        size = ham.shape[0] // hparts
        window = pl.ds(c * size, size)
        hc = pltpu.make_async_copy(ham_hbm.at[window], ham.at[window], ham_sem.at[c])
        hc.start()
        hcopies.append(hc)

    barrier = pltpu.get_barrier_semaphore()
    peers = [{"elem": left}, {"elem": right}]
    for j in range(1, nband):
        peers.append({"band": lax.rem(bme + j, nband)})
    for j in range(1, n1):
        peers.append({"elem": group * n1 + lax.rem(member + j, n1)})
    for j in range(1, n2):
        peers.append({"elem": lax.rem(group + j, n2) * n1 + member})
    for peer in peers:
        pl.semaphore_signal(barrier, inc=1, device_id=peer, device_id_type=MESH)
    pl.semaphore_wait(barrier, len(peers))

    core = me % 2
    near_base, far_base = (1 - core) * cells, core * cells
    near_face, far_face = 6 - core, 5 + core
    near_peer = me + 1 - 2 * core
    far_peer = lax.rem(me + n - 1 + 2 * core, n)
    nears, fars = (near0, near1), (far0, far1)
    piece = cells // FAR

    def near_copy(step, source):
        return pltpu.make_async_remote_copy(
            src_ref=source.at[pl.ds(near_base, cells)],
            dst_ref=nears[step % 2],
            send_sem=near_send.at[step],
            recv_sem=near_recv.at[step],
            device_id={"elem": near_peer},
            device_id_type=MESH,
        )

    def far_copy(step, source, c):
        return pltpu.make_async_remote_copy(
            src_ref=source.at[pl.ds(far_base + c * piece, piece)],
            dst_ref=fars[step % 2].at[pl.ds(c * piece, piece)],
            send_sem=far_send.at[step, c],
            recv_sem=far_recv.at[step, c],
            device_id={"elem": far_peer},
            device_id_type=MESH,
        )

    fcopies = []

    def send_field(layer, base):
        window = pl.ds(base, cells)
        for j in range(1, nband):
            copy = pltpu.make_async_remote_copy(
                src_ref=buf_a.at[window],
                dst_ref=others.at[j - 1, layer],
                send_sem=fsend.at[j - 1, layer],
                recv_sem=frecv.at[j - 1, layer],
                device_id={"band": lax.rem(bme + j, nband)},
                device_id_type=MESH,
            )
            copy.start()
            fcopies.append((j, layer, copy))

    late = (member == 0) | (member == n1 - 1)
    near = near_copy(0, y0)
    far = [far_copy(0, y0, c) for c in range(FAR)]

    @pl.when(jnp.logical_not(late))
    def _():
        for copy in far:
            copy.start()

    near.start()
    for c, hc in enumerate(hcopies):
        hc.wait()
        if c == LATE:

            @pl.when(late)
            def _():
                for copy in far:
                    copy.start()

    current = y0
    for step in range(DEGREE + 1):
        last = step == DEGREE
        target = buf_b if step % 2 == 0 else buf_a
        prior = y0 if step == 1 else target

        def local(e, carry, current=current):
            layer, cell = e // cells, e % cells
            base, own = e * 7, layer * cells
            total_ = dot(ham[base], current[e])
            for d in range(4):
                total_ += dot(
                    ham[base + d + 1], current[own + lax.rem(nbr[d, layer, cell], cells)]
                )
            there = cells - own + lax.rem(nbr[5 - layer, layer, cell], cells)
            total_ += dot(ham[base + 6 - layer], current[there])
            acc[e] = total_
            return carry

        lax.fori_loop(0, total, local, 0, unroll=4)

        def finish(i, carry, halo, base, face, step=step, target=target, prior=prior):
            e = base + i
            index = lax.rem(nbr[face - 1, base // cells, i], cells)
            value = acc[e] + dot(ham[e * 7 + face], halo[index])
            if step > 0 and step < DEGREE:
                value = 2.0 * value - prior[e].astype(F32)
            if step < DEGREE:
                target[e] = value.astype(BF16)
            else:
                it[e] = value.T.astype(BF16)
            return carry

        near.wait_recv()
        at_near = functools.partial(
            finish, halo=nears[step % 2], base=near_base, face=near_face
        )
        at_far = functools.partial(
            finish, halo=fars[step % 2], base=far_base, face=far_face
        )
        near_next, far_next = None, []
        lax.fori_loop(0, cells, at_near, 0, unroll=4)
        if not last:
            near_next = near_copy(step + 1, target)
            near_next.start()
        if step == DEGREE - 1:
            send_field(0, near_base)
        for copy in far:
            copy.wait_recv()
        if last:
            lax.fori_loop(0, cells, at_far, 0, unroll=4)
        else:
            for c in range(FAR):
                lax.fori_loop(c * piece, (c + 1) * piece, at_far, 0, unroll=4)
                copy = far_copy(step + 1, target, c)
                copy.start()
                far_next.append(copy)
        if step == DEGREE - 1:
            send_field(1, far_base)
            written = pltpu.make_async_copy(buf_a, f_out, out_sem)
            written.start()

            def turn(e, carry):
                ft[e] = buf_a[e].astype(F32).T.astype(BF16)
                return carry

            lax.fori_loop(0, total, turn, 0, unroll=4)
        near.wait_send()
        for copy in far:
            copy.wait_send()
        near, far = near_next, far_next
        current = target

    per = bands // rows

    def gram(field, first, count, state):
        def body(i, carry):
            s, p = carry
            v = field(i)
            e = first + i
            return s + dot(ft[e], v), p + dot(it[e], v)

        return lax.fori_loop(0, count, body, state, unroll=4)

    def put(who, state):
        for t in range(2):
            block = state[t].T.reshape(per, rows, bands)
            for i in range(per):
                r = who * per + i
                parts[r % n1, r // n1, t] = block[i]

    zero = jnp.zeros((bands, bands), F32)
    put(bme, gram(lambda e: buf_a[e], 0, total, (zero, zero)))
    for j in range(1, nband):
        state = (zero, zero)
        for jj, layer, copy in fcopies:
            if jj == j:
                copy.wait_recv()
                base = near_base if layer == 0 else far_base
                state = gram(lambda i: others[j - 1, layer, i], base, cells, state)
        put(lax.rem(bme + nband - j, nband), state)

    copies = []
    for j in range(1, n1):
        to = lax.rem(member + j, n1)
        copy = pltpu.make_async_remote_copy(
            src_ref=parts.at[to],
            dst_ref=got1.at[j - 1],
            send_sem=r1send.at[j - 1],
            recv_sem=r1recv.at[j - 1],
            device_id={"elem": group * n1 + to},
            device_id_type=MESH,
        )
        copy.start()
        copies.append(copy)
    for _, _, copy in fcopies:
        copy.wait_send()
    running = parts[member]
    for j, copy in enumerate(copies):
        copy.wait_recv()
        running += got1[j]
    mid[...] = running
    copies2 = []
    for j in range(1, n2):
        to = lax.rem(group + j, n2)
        copy = pltpu.make_async_remote_copy(
            src_ref=mid.at[to],
            dst_ref=got2.at[j - 1],
            send_sem=r2send.at[j - 1],
            recv_sem=r2recv.at[j - 1],
            device_id={"elem": to * n1 + member},
            device_id_type=MESH,
        )
        copy.start()
        copies2.append(copy)
    for copy in copies:
        copy.wait_send()
    final = mid[group]
    for j, copy in enumerate(copies2):
        copy.wait_recv()
        final += got2[j]
    for copy in copies2:
        copy.wait_send()
    written.wait()
    s_out[...] = final[0] * factor
    p_out[...] = final[1] * factor


def body(n, nband, basis, hamiltonian, neighbours):
    bands, layers, cells, funcs = basis.shape
    total = layers * cells
    depth = layers * n
    rows = bands * nband // n
    n1 = 4
    n2 = n // n1
    nbr = neighbours.transpose(2, 0, 1)
    y0 = basis.reshape(bands, total, funcs).transpose(1, 2, 0)
    ham = hamiltonian.reshape(total * 7, funcs, funcs)
    factor = 1.0 / (depth * cells * funcs)
    geom = (n, nband, cells, n1, n2, rows, factor)
    vm = pl.BlockSpec(memory_space=pltpu.VMEM)
    half = (cells, funcs, bands)
    dma = pltpu.SemaphoreType.DMA
    small = jax.ShapeDtypeStruct((rows, bands), F32)
    field, s, p = pl.pallas_call(
        functools.partial(kernel, geom),
        out_shape=(jax.ShapeDtypeStruct((total, funcs, bands), BF16), small, small),
        in_specs=[
            pl.BlockSpec(memory_space=pltpu.SMEM),
            vm,
            pl.BlockSpec(memory_space=pl.ANY),
        ],
        out_specs=(pl.BlockSpec(memory_space=pl.ANY), vm, vm),
        scratch_shapes=[
            pltpu.VMEM((total * 7, funcs, funcs), BF16),
            pltpu.VMEM((total, funcs, bands), BF16),
            pltpu.VMEM((total, funcs, bands), BF16),
            pltpu.VMEM(half, BF16),
            pltpu.VMEM(half, BF16),
            pltpu.VMEM(half, BF16),
            pltpu.VMEM(half, BF16),
            pltpu.VMEM((total, funcs, bands), F32),
            pltpu.VMEM((total, bands, funcs), BF16),
            pltpu.VMEM((total, bands, funcs), BF16),
            pltpu.VMEM((nband - 1, 2, cells, funcs, bands), BF16),
            pltpu.VMEM((n1, n2, 2, rows, bands), F32),
            pltpu.VMEM((n1 - 1, n2, 2, rows, bands), F32),
            pltpu.VMEM((n2, 2, rows, bands), F32),
            pltpu.VMEM((n2 - 1, 2, rows, bands), F32),
            dma((4,)),
            dma,
            dma((DEGREE + 1,)),
            dma((DEGREE + 1,)),
            dma((DEGREE + 1, FAR)),
            dma((DEGREE + 1, FAR)),
            dma((nband - 1, 2)),
            dma((nband - 1, 2)),
            dma((n1 - 1,)),
            dma((n1 - 1,)),
            dma((n2 - 1,)),
            dma((n2 - 1,)),
        ],
        compiler_params=pltpu.CompilerParams(
            collective_id=0, has_side_effects=True, vmem_limit_bytes=56 * 1024 * 1024
        ),
    )(nbr, y0, ham)
    filtered = field.transpose(2, 0, 1).reshape(bands, layers, cells, funcs)
    return filtered, s, p


def solution(mesh):
    placed = (
        P("band", "elem", None, None),
        P("elem", None, None, None, None),
        P("elem", None, None),
    )
    return jax.shard_map(
        functools.partial(body, mesh.shape["elem"], mesh.shape["band"]),
        mesh=mesh,
        in_specs=placed,
        out_specs=(P("band", "elem", None, None), P("elem", "band"), P("elem", "band")),
        check_vma=False,
    )
```

profile of v0, /device:TPU:0, one launch (start us, length us, event | category | flops | bytes accessed | tf_op | source)
XLA Modules:
  0.0 107.3 jit_solution(13896115046468341341)
XLA Ops:
  0.6 103.0 %shard_map.58 = (bf16[32,160,128]{2,1,0:T(8,128)(2,1)}, f32[16,128]{1,0:T(8,128)}, f32[16,128]{1,0:T(8,128)}) custom-call(s32[6,2,16]{2,1,0:T(2,128)} %bitcast.11, bf16[32,160,128]{2,1,0:T(8,128)(2,1)} %bitcast.9, bf16[224,160,160]{2,1,0:T(8,128)(2,1)} %bitcast.8), custom_call_target="tpu_custom_call" | custom-call | tf_op jit(solution)/shard_map/pallas_call | solution.py:314
  103.7 0.0 copy-start.1
  103.7 0.0 copy-start
  103.7 2.5 %copy.9 = bf16[128,2,16,160]{0,3,2,1:T(8,128)(2,1)} copy(bf16[128,2,16,160]{0,3,2,1:T(8,128)(2,1)} %bitcast.10) | data formatting | bytes 2621440
  106.1 0.0 copy-done.1
  106.1 0.6 copy.10
  106.7 0.0 copy-done
  106.7 0.6 copy.11
Async XLA Ops:
  103.7 2.5 %copy-start.1 = (f32[16,128]{1,0:T(8,128)S(1)}, f32[16,128]{1,0:T(8,128)}, u32[]{:S(2)}) copy-start(f32[16,128]{1,0:T(8,128)} %get-tuple-element.13) | copy-start | bytes 24580
  103.7 3.1 %copy-start = (f32[16,128]{1,0:T(8,128)S(1)}, f32[16,128]{1,0:T(8,128)}, u32[]{:S(2)}) copy-start(f32[16,128]{1,0:T(8,128)} %get-tuple-element.14) | copy-start | bytes 24580
where the time goes:
time: 108 us; the launch traced here: 107 us
  Pallas kernels  103 us (95%)
  local copies, waits for them, and re-layouts  3.67 us (3%)
    pallas_call x1, Pallas kernels, body(): pl.pallas_call(functools.partial(kernel, geom), out_shape=(jax.ShapeDtype...  103 us
    unnamed x7, local copies, waits for them, and re-layouts  3.67 us

commit v1 on v0

v1 whole, which is shorter than its diff:
```python
import functools

import jax
import jax.numpy as jnp
from jax import lax
from jax.experimental import pallas as pl
from jax.experimental.pallas import tpu as pltpu
from jax.sharding import PartitionSpec as P

DEGREE = 4
PIECES = 4
MESH = pl.DeviceIdType.MESH
F32 = jnp.float32
BF16 = jnp.bfloat16


def dot(a, b):
    return jnp.dot(a, b, preferred_element_type=F32)


def kernel(
    geom,
    nbr,
    y0_hbm,
    ham_hbm,
    f_out,
    s_out,
    p_out,
    ham,
    y0,
    buf_a,
    buf_b,
    near0,
    near1,
    far0,
    far1,
    stage0,
    stage1,
    ordered,
    fi,
    sums,
    others,
    parts,
    got1,
    mid,
    got2,
    tab,
    ham_sem,
    y0_sem,
    out_sem,
    near_send,
    near_recv,
    far_send,
    far_recv,
    fsend,
    frecv,
    r1send,
    r1recv,
    r2send,
    r2recv,
):
    n, nband, cells, n1, n2, rows, factor = geom
    total = 2 * cells
    bands = y0.shape[2]
    me = lax.axis_index("elem")
    bme = lax.axis_index("band")
    right, left = lax.rem(me + 1, n), lax.rem(me + n - 1, n)
    group, member = me // n1, me % n1

    first = pltpu.make_async_copy(y0_hbm, y0, y0_sem)
    first.start()
    hcopies = []
    hparts = ham_sem.shape[0]
    for c in range(hparts):
        size = ham.shape[0] // hparts
        window = pl.ds(c * size, size)
        hc = pltpu.make_async_copy(ham_hbm.at[window], ham.at[window], ham_sem.at[c])
        hc.start()
        hcopies.append(hc)

    barrier = pltpu.get_barrier_semaphore()
    peers = [{"elem": left}, {"elem": right}]
    for j in range(1, nband):
        peers.append({"band": lax.rem(bme + j, nband)})
    for j in range(1, n1):
        peers.append({"elem": group * n1 + lax.rem(member + j, n1)})
    for j in range(1, n2):
        peers.append({"elem": lax.rem(group + j, n2) * n1 + member})
    for peer in peers:
        pl.semaphore_signal(barrier, inc=1, device_id=peer, device_id_type=MESH)

    core = me % 2
    near_base, far_base = (1 - core) * cells, core * cells
    near_peer = me + 1 - 2 * core
    far_peer = lax.rem(me + n - 1 + 2 * core, n)
    nears, fars, stages = (near0, near1), (far0, far1), (stage0, stage1)
    piece = cells // PIECES

    down = [lax.rem(nbr[4, 0, c], cells) for c in range(cells)]
    for c in range(cells):
        tab[6, far_base + c] = far_base + jnp.where(core == 0, down[c], c)

    def far_slots(i, carry):
        cell = jnp.int32(0)
        for c in range(cells):
            cell = jnp.where(down[c] == i, c, cell)
        cell = jnp.where(core == 0, cell, i)
        tab[0, far_base + i] = far_base + cell
        return carry

    lax.fori_loop(0, cells, far_slots, 0)

    def near_slots(i, carry):
        above = lax.rem(nbr[4 + core, 1 - core, i], cells)
        tab[6, near_base + i] = tab[6, far_base + above] - far_base + near_base
        cell = lax.rem(nbr[5 - core, core, tab[0, far_base + i] - far_base], cells)
        tab[0, near_base + i] = near_base + cell
        tab[5, near_base + i] = lax.rem(nbr[5 - core, 1 - core, cell], cells)
        return carry

    lax.fori_loop(0, cells, near_slots, 0)
    first.wait()

    def order(i, carry):
        buf_b[far_base + i] = y0[tab[0, far_base + i]]
        return carry

    lax.fori_loop(0, cells, order, 0, unroll=4)
    pl.semaphore_wait(barrier, len(peers))

    def near_copy(step):
        source = y0.at[pl.ds(near_base, cells)] if step == 0 else stages[step % 2]
        return pltpu.make_async_remote_copy(
            src_ref=source,
            dst_ref=nears[step % 2],
            send_sem=near_send.at[step],
            recv_sem=near_recv.at[step],
            device_id={"elem": near_peer},
            device_id_type=MESH,
        )

    def far_copy(step, p):
        source = buf_b if step % 2 == 0 else buf_a
        return pltpu.make_async_remote_copy(
            src_ref=source.at[pl.ds(far_base + p * piece, piece)],
            dst_ref=fars[step % 2].at[pl.ds(p * piece, piece)],
            send_sem=far_send.at[step, p],
            recv_sem=far_recv.at[step, p],
            device_id={"elem": far_peer},
            device_id_type=MESH,
        )

    def field_copy(j, layer, p):
        base = near_base if layer == 0 else far_base
        return pltpu.make_async_remote_copy(
            src_ref=buf_b.at[pl.ds(base + p * piece, piece)],
            dst_ref=others.at[j - 1, layer, pl.ds(p * piece, piece)],
            send_sem=fsend.at[j - 1, layer, p],
            recv_sem=frecv.at[j - 1, layer, p],
            device_id={"band": lax.rem(bme + j, nband)},
            device_id_type=MESH,
        )

    for p in range(PIECES):
        far_copy(0, p).start()
    near_copy(0).start()

    def order_near(i, carry):
        buf_b[near_base + i] = y0[tab[0, near_base + i]]
        return carry

    lax.fori_loop(0, cells, order_near, 0, unroll=4)

    def layer_slots(i, carry):
        for layer in range(2):
            own = layer * cells
            cell = tab[0, own + i] - own
            for d in range(4):
                other = lax.rem(nbr[d, layer, cell], cells)
                tab[1 + d, own + i] = tab[6, own + other]
        return carry

    lax.fori_loop(0, cells, layer_slots, 0)
    for t in range(nband):
        sums[t] = jnp.zeros(sums.shape[1:], F32)
    for hc in hcopies:
        hc.wait()

    def gram(t, slot, field):
        sums[t] += sum(dot(fi[slot + i], field(i)) for i in range(piece))

    def gram_own(base, p):
        gram(0, base + p * piece, lambda i: buf_b[base + p * piece + i])

    def gram_other(j, layer, p):
        base = near_base if layer == 0 else far_base
        field_copy(j, layer, p).wait_recv()
        gram(j, base + p * piece, lambda i: others[j - 1, layer, p * piece + i])

    written = pltpu.make_async_copy(ordered, f_out, out_sem)
    for step in range(DEGREE + 1):
        last = step == DEGREE
        current, target = (buf_b, buf_a) if step % 2 == 0 else (buf_a, buf_b)
        near_halo, far_halo = nears[step % 2], fars[step % 2]

        def cell(base, i, straight, halo, step=step, current=current, target=target):
            slot = base + i
            block = tab[0, slot] * 7
            value = dot(ham[block], current[slot])
            for d in range(4):
                value += dot(ham[block + d + 1], current[tab[1 + d, slot]])
            value += dot(ham[block + straight], current[near_base + far_base - base + i])
            value += dot(ham[block + 11 - straight], halo)
            if step > 0 and step < DEGREE:
                value = 2.0 * value - target[slot].astype(F32)
            if step < DEGREE:
                target[slot] = value.astype(BF16)
            if step == DEGREE - 1:
                fi[slot, :bands] = value.T.astype(BF16)
            if step == DEGREE:
                fi[slot, bands:] = value.T.astype(BF16)

        near_copy(step).wait_recv()

        def do(
            p,
            carry,
            step=step,
            last=last,
            target=target,
            near_halo=near_halo,
            far_halo=far_halo,
            cell=cell,
        ):
            for t in range(piece):
                i = p * piece + t
                cell(near_base, i, 5 + core, near_halo[tab[5, near_base + i]])
            if step == DEGREE - 1:
                for j in range(1, nband):
                    field_copy(j, 0, p).start()
            if not last:

                @pl.when(p == PIECES - 1)
                def _():
                    if step > 0:
                        near_copy(step - 1).wait_send()

                    def put_near(i, carry):
                        stages[(step + 1) % 2][i] = target[tab[6, near_base + i]]
                        return carry

                    lax.fori_loop(0, cells, put_near, 0, unroll=4)
                    near_copy(step + 1).start()

            else:
                share = total // PIECES

                def put_out(i, carry):
                    ordered[p * share + i] = buf_b[tab[6, p * share + i]]
                    return carry

                lax.fori_loop(0, share, put_out, 0, unroll=4)
                gram_own(near_base, p)

                @pl.when(p > 0)
                def _():
                    for j in range(1, nband):
                        for layer in range(2):
                            gram_other(j, layer, p - 1)

            far_copy(step, p).wait_recv()
            if step > 0:
                far_copy(step - 1, p).wait_send()
            for t in range(piece):
                i = p * piece + t
                cell(far_base, i, 6 - core, far_halo[i])
            if not last:
                far_copy(step + 1, p).start()
            if step == DEGREE - 1:
                for j in range(1, nband):
                    field_copy(j, 1, p).start()
            if last:
                gram_own(far_base, p)
            return carry

        lax.fori_loop(0, PIECES, do, 0)
    written.start()
    near_copy(DEGREE - 1).wait_send()
    near_copy(DEGREE).wait_send()
    for p in range(PIECES):
        far_copy(DEGREE, p).wait_send()
    for j in range(1, nband):
        for layer in range(2):
            gram_other(j, layer, PIECES - 1)

    per = bands // rows

    def put(who, t):
        for u in range(2):
            block = sums[t, u * bands : (u + 1) * bands].T.reshape(per, rows, bands)
            for i in range(per):
                r = who * per + i
                parts[r % n1, r // n1, u] = block[i]

    put(bme, 0)
    for j in range(1, nband):
        put(lax.rem(bme + nband - j, nband), j)

    copies = []
    for j in range(1, n1):
        to = lax.rem(member + j, n1)
        copy = pltpu.make_async_remote_copy(
            src_ref=parts.at[to],
            dst_ref=got1.at[j - 1],
            send_sem=r1send.at[j - 1],
            recv_sem=r1recv.at[j - 1],
            device_id={"elem": group * n1 + to},
            device_id_type=MESH,
        )
        copy.start()
        copies.append(copy)
    for j in range(1, nband):
        for layer in range(2):
            for p in range(PIECES):
                field_copy(j, layer, p).wait_send()
    running = parts[member]
    for j, copy in enumerate(copies):
        copy.wait_recv()
        running += got1[j]
    mid[...] = running
    copies2 = []
    for j in range(1, n2):
        to = lax.rem(group + j, n2)
        copy = pltpu.make_async_remote_copy(
            src_ref=mid.at[to],
            dst_ref=got2.at[j - 1],
            send_sem=r2send.at[j - 1],
            recv_sem=r2recv.at[j - 1],
            device_id={"elem": to * n1 + member},
            device_id_type=MESH,
        )
        copy.start()
        copies2.append(copy)
    for copy in copies:
        copy.wait_send()
    final = mid[group]
    for j, copy in enumerate(copies2):
        copy.wait_recv()
        final += got2[j]
    for copy in copies2:
        copy.wait_send()
    written.wait()
    s_out[...] = final[0] * factor
    p_out[...] = final[1] * factor


def body(n, nband, basis, hamiltonian, neighbours):
    bands, layers, cells, funcs = basis.shape
    total = layers * cells
    depth = layers * n
    rows = bands * nband // n
    n1 = 4
    n2 = n // n1
    nbr = neighbours.transpose(2, 0, 1)
    y0 = basis.reshape(bands, total, funcs).transpose(1, 2, 0)
    ham = hamiltonian.reshape(total * 7, funcs, funcs)
    factor = 1.0 / (depth * cells * funcs)
    geom = (n, nband, cells, n1, n2, rows, factor)
    vm = pl.BlockSpec(memory_space=pltpu.VMEM)
    half = (cells, funcs, bands)
    dma = pltpu.SemaphoreType.DMA
    small = jax.ShapeDtypeStruct((rows, bands), F32)
    field, s, p = pl.pallas_call(
        functools.partial(kernel, geom),
        out_shape=(jax.ShapeDtypeStruct((total, funcs, bands), BF16), small, small),
        in_specs=[
            pl.BlockSpec(memory_space=pltpu.SMEM),
            pl.BlockSpec(memory_space=pl.ANY),
            pl.BlockSpec(memory_space=pl.ANY),
        ],
        out_specs=(pl.BlockSpec(memory_space=pl.ANY), vm, vm),
        scratch_shapes=[
            pltpu.VMEM((total * 7, funcs, funcs), BF16),
            pltpu.VMEM((total, funcs, bands), BF16),
            pltpu.VMEM((total, funcs, bands), BF16),
            pltpu.VMEM((total, funcs, bands), BF16),
            pltpu.VMEM(half, BF16),
            pltpu.VMEM(half, BF16),
            pltpu.VMEM(half, BF16),
            pltpu.VMEM(half, BF16),
            pltpu.VMEM(half, BF16),
            pltpu.VMEM(half, BF16),
            pltpu.VMEM((total, funcs, bands), BF16),
            pltpu.VMEM((total, 2 * bands, funcs), BF16),
            pltpu.VMEM((nband, 2 * bands, bands), F32),
            pltpu.VMEM((nband - 1, 2, cells, funcs, bands), BF16),
            pltpu.VMEM((n1, n2, 2, rows, bands), F32),
            pltpu.VMEM((n1 - 1, n2, 2, rows, bands), F32),
            pltpu.VMEM((n2, 2, rows, bands), F32),
            pltpu.VMEM((n2 - 1, 2, rows, bands), F32),
            pltpu.SMEM((7, total), jnp.int32),
            dma((4,)),
            dma,
            dma,
            dma((DEGREE + 1,)),
            dma((DEGREE + 1,)),
            dma((DEGREE + 1, PIECES)),
            dma((DEGREE + 1, PIECES)),
            dma((nband - 1, 2, PIECES)),
            dma((nband - 1, 2, PIECES)),
            dma((n1 - 1,)),
            dma((n1 - 1,)),
            dma((n2 - 1,)),
            dma((n2 - 1,)),
        ],
        compiler_params=pltpu.CompilerParams(
            collective_id=0, has_side_effects=True, vmem_limit_bytes=56 * 1024 * 1024
        ),
    )(nbr, y0, ham)
    filtered = field.transpose(2, 0, 1).reshape(bands, layers, cells, funcs)
    return filtered, s, p


def solution(mesh):
    placed = (
        P("band", "elem", None, None),
        P("elem", None, None, None, None),
        P("elem", None, None),
    )
    return jax.shard_map(
        functools.partial(body, mesh.shape["elem"], mesh.shape["band"]),
        mesh=mesh,
        in_specs=placed,
        out_specs=(P("band", "elem", None, None), P("elem", "band"), P("elem", "band")),
        check_vma=False,
    )
```

time: 108 us -> 106 us (0.981)
    pallas_call x1, Pallas kernels: 103 us -> 102 us  [body(): pl.pallas_call(functools.partial(kernel, geom), out_shape=(jax.ShapeDtype...]
where the time goes in v1:
time: 106 us
  Pallas kernels  102 us (96%)
  local copies, waits for them, and re-layouts  3.67 us (3%)
    pallas_call x1, Pallas kernels, body(): pl.pallas_call(functools.partial(kernel, geom), out_shape=(jax.ShapeDtype...  102 us
    unnamed x7, local copies, waits for them, and re-layouts  3.67 us

profile of v1, /device:TPU:0, one launch (start us, length us, event | category | flops | bytes accessed | tf_op | source)
XLA Modules:
  0.0 106.2 jit_solution(2274093095019035171)
XLA Ops:
  0.6 101.9 %shard_map.58 = (bf16[32,160,128]{2,1,0:T(8,128)(2,1)}, f32[16,128]{1,0:T(8,128)}, f32[16,128]{1,0:T(8,128)}) custom-call(s32[6,2,16]{2,1,0:T(2,128)} %bitcast.11, bf16[32,160,128]{2,1,0:T(8,128)(2,1)} %bitcast.9, bf16[224,160,160]{2,1,0:T(8,128)(2,1)} %bitcast.8), custom_call_target="tpu_custom_call" | custom-call | tf_op jit(solution)/shard_map/pallas_call | solution.py:373
  102.5 0.0 copy-start.1
  102.6 0.0 copy-start
  102.6 2.5 %copy.9 = bf16[128,2,16,160]{0,3,2,1:T(8,128)(2,1)} copy(bf16[128,2,16,160]{0,3,2,1:T(8,128)(2,1)} %bitcast.10) | data formatting | bytes 2621440
  105.0 0.0 copy-done.1
  105.0 0.6 copy.10
  105.6 0.0 copy-done
  105.6 0.6 copy.11
Async XLA Ops:
  102.5 2.5 %copy-start.1 = (f32[16,128]{1,0:T(8,128)S(1)}, f32[16,128]{1,0:T(8,128)}, u32[]{:S(2)}) copy-start(f32[16,128]{1,0:T(8,128)} %get-tuple-element.13) | copy-start | bytes 24580
  102.6 3.1 %copy-start = (f32[16,128]{1,0:T(8,128)S(1)}, f32[16,128]{1,0:T(8,128)}, u32[]{:S(2)}) copy-start(f32[16,128]{1,0:T(8,128)} %get-tuple-element.14) | copy-start | bytes 24580

commit v2 on v1

--- a/solution.py
+++ b/solution.py
@@ -37,6 +37,7 @@
     stage0,
     stage1,
     ordered,
+    acc,
     fi,
     sums,
     others,
@@ -203,14 +204,18 @@
         current, target = (buf_b, buf_a) if step % 2 == 0 else (buf_a, buf_b)
         near_halo, far_halo = nears[step % 2], fars[step % 2]
 
-        def cell(base, i, straight, halo, step=step, current=current, target=target):
+        def local(base, i, straight, current=current):
             slot = base + i
             block = tab[0, slot] * 7
             value = dot(ham[block], current[slot])
             for d in range(4):
                 value += dot(ham[block + d + 1], current[tab[1 + d, slot]])
-            value += dot(ham[block + straight], current[near_base + far_base - base + i])
-            value += dot(ham[block + 11 - straight], halo)
+            across = near_base + far_base - base + i
+            return value + dot(ham[block + straight], current[across])
+
+        def finish(base, i, face, value, halo, step=step, target=target):
+            slot = base + i
+            value += dot(ham[tab[0, slot] * 7 + face], halo)
             if step > 0 and step < DEGREE:
                 value = 2.0 * value - target[slot].astype(F32)
             if step < DEGREE:
@@ -220,7 +225,18 @@
             if step == DEGREE:
                 fi[slot, bands:] = value.T.astype(BF16)
 
-        near_copy(step).wait_recv()
+        def near_piece(
+            p, step=step, near_halo=near_halo, local=local, finish=finish, last=last
+        ):
+            for t in range(piece):
+                i = p * piece + t
+                halo = near_halo[tab[5, near_base + i]]
+                finish(near_base, i, 6 - core, local(near_base, i, 5 + core), halo)
+            if step == DEGREE - 1:
+                for j in range(1, nband):
+                    field_copy(j, 0, p).start()
+            if last:
+                gram_own(near_base, p)
 
         def do(
             p,
@@ -228,16 +244,22 @@
             step=step,
             last=last,
             target=target,
-            near_halo=near_halo,
             far_halo=far_halo,
-            cell=cell,
+            local=local,
+            finish=finish,
+            near_piece=near_piece,
         ):
             for t in range(piece):
-                i = p * piece + t
-                cell(near_base, i, 5 + core, near_halo[tab[5, near_base + i]])
-            if step == DEGREE - 1:
-                for j in range(1, nband):
-                    field_copy(j, 0, p).start()
+                acc[t] = local(far_base, p * piece + t, 6 - core)
+
+            @pl.when(p > 0)
+            def _():
+                near_piece(p)
+                if last:
+                    for j in range(1, nband):
+                        for layer in range(2):
+                            gram_other(j, layer, p - 1)
+
             if not last:
 
                 @pl.when(p == PIECES - 1)
@@ -251,29 +273,13 @@
 
                     lax.fori_loop(0, cells, put_near, 0, unroll=4)
                     near_copy(step + 1).start()
-
-            else:
-                share = total // PIECES
-
-                def put_out(i, carry):
-                    ordered[p * share + i] = buf_b[tab[6, p * share + i]]
-                    return carry
-
-                lax.fori_loop(0, share, put_out, 0, unroll=4)
-                gram_own(near_base, p)
-
-                @pl.when(p > 0)
-                def _():
-                    for j in range(1, nband):
-                        for layer in range(2):
-                            gram_other(j, layer, p - 1)
 
             far_copy(step, p).wait_recv()
             if step > 0:
                 far_copy(step - 1, p).wait_send()
             for t in range(piece):
                 i = p * piece + t
-                cell(far_base, i, 6 - core, far_halo[i])
+                finish(far_base, i, 5 + core, acc[t], far_halo[i])
             if not last:
                 far_copy(step + 1, p).start()
             if step == DEGREE - 1:
@@ -281,10 +287,23 @@
                     field_copy(j, 1, p).start()
             if last:
                 gram_own(far_base, p)
+
+            @pl.when(p == 0)
+            def _():
+                near_copy(step).wait_recv()
+                near_piece(p)
+                if last:
+
+                    def put_out(e, carry):
+                        ordered[e] = buf_b[tab[6, e]]
+                        return carry
+
+                    lax.fori_loop(0, total, put_out, 0, unroll=4)
+                    written.start()
+
             return carry
 
         lax.fori_loop(0, PIECES, do, 0)
-    written.start()
     near_copy(DEGREE - 1).wait_send()
     near_copy(DEGREE).wait_send()
     for p in range(PIECES):
@@ -354,6 +373,14 @@
     p_out[...] = final[1] * factor
 
 
+def copy_kernel(field, s, p, f_out, s_out, p_out, sem):
+    copy = pltpu.make_async_copy(field, f_out, sem)
+    copy.start()
+    s_out[...] = s[...]
+    p_out[...] = p[...]
+    copy.wait()
+
+
 def body(n, nband, basis, hamiltonian, neighbours):
     bands, layers, cells, funcs = basis.shape
     total = layers * cells
@@ -391,6 +418,7 @@
             pltpu.VMEM(half, BF16),
             pltpu.VMEM(half, BF16),
             pltpu.VMEM((total, funcs, bands), BF16),
+            pltpu.VMEM((cells // PIECES, funcs, bands), F32),
             pltpu.VMEM((total, 2 * bands, funcs), BF16),
             pltpu.VMEM((nband, 2 * bands, bands), F32),
             pltpu.VMEM((nband - 1, 2, cells, funcs, bands), BF16),
@@ -417,6 +445,14 @@
             collective_id=0, has_side_effects=True, vmem_limit_bytes=56 * 1024 * 1024
         ),
     )(nbr, y0, ham)
+    field, s, p = pl.pallas_call(
+        copy_kernel,
+        out_shape=(jax.ShapeDtypeStruct((total, funcs, bands), BF16), small, small),
+        in_specs=[vm, vm, vm],
+        out_specs=(pl.BlockSpec(memory_space=pl.ANY), vm, vm),
+        scratch_shapes=[dma],
+        compiler_params=pltpu.CompilerParams(vmem_limit_bytes=8 * 1024 * 1024),
+    )(field, s, p)
     filtered = field.transpose(2, 0, 1).reshape(bands, layers, cells, funcs)
     return filtered, s, p
 

time: 106 us -> 108 us (1.019)
  Pallas kernels: 102 us -> 104 us
    pallas_call x0 -> x1, Pallas kernels: none -> 1.67 us  [body(): pl.pallas_call(copy_kernel, out_shape=(jax.ShapeDtypeStruct((total, funcs...]
    unnamed x7 -> x6, local copies, waits for them, and re-layouts: 3.67 us -> 2.7 us
where the time goes in v2:
time: 108 us; the launch traced here: 107 us
  Pallas kernels  104 us (96%)
  local copies, waits for them, and re-layouts  2.7 us (2%)
    pallas_call x1, Pallas kernels, body(): pl.pallas_call(functools.partial(kernel, geom), out_shape=(jax.ShapeDtype...  102 us
    unnamed x6, local copies, waits for them, and re-layouts  2.7 us

profile of v2, /device:TPU:0, one launch (start us, length us, event | category | flops | bytes accessed | tf_op | source)
XLA Modules:
  0.0 107.3 jit_solution(10423667569556710569)
XLA Ops:
  0.6 102.3 %shard_map.58 = (bf16[32,160,128]{2,1,0:T(8,128)(2,1)}, f32[16,128]{1,0:T(8,128)}, f32[16,128]{1,0:T(8,128)}) custom-call(s32[6,2,16]{2,1,0:T(2,128)} %bitcast.10, bf16[32,160,128]{2,1,0:T(8,128)(2,1)} %bitcast.9, bf16[224,160,160]{2,1,0:T(8,128)(2,1)} %bitcast.8), custom_call_target="tpu_custom_call" | custom-call | tf_op jit(solution)/shard_map/pallas_call | solution.py:400
  103.0 0.0 copy-start
  103.0 1.3 %copy-done = bf16[32,160,128]{2,1,0:T(8,128)(2,1)S(1)} copy-done((bf16[32,160,128]{2,1,0:T(8,128)(2,1)S(1)}, bf16[32,160,128]{2,1,0:T(8,128)(2,1)}, u32[]{:S(2)}) %copy-start) | copy-done | bytes 1310744
  104.3 0.0 copy-start.1
  104.3 0.7 copy-done.1
  105.0 0.0 copy-start.2
  105.0 0.7 copy-done.2
  105.7 1.7 %shard_map.59 = (bf16[32,160,128]{2,1,0:T(8,128)(2,1)}, f32[16,128]{1,0:T(8,128)}, f32[16,128]{1,0:T(8,128)}) custom-call(bf16[32,160,128]{2,1,0:T(8,128)(2,1)S(1)} %copy-done, f32[16,128]{1,0:T(8,128)S(1)} %copy-done.1, f32[16,128]{1,0:T(8,128)S(1)} %copy-done.2), custom_call_target="tpu_custom_call" | custom-call | tf_op jit(solution)/shard_map/pallas_call | solution.py:448
Async XLA Ops:
  103.0 1.3 %copy-start = (bf16[32,160,128]{2,1,0:T(8,128)(2,1)S(1)}, bf16[32,160,128]{2,1,0:T(8,128)(2,1)}, u32[]{:S(2)}) copy-start(bf16[32,160,128]{2,1,0:T(8,128)(2,1)} %get-tuple-element.9.field) | copy-start | bytes 3932164
  104.3 0.7 copy-start.1
  105.0 0.7 copy-start.2
